TPU v7x, 128 devices: a whole 4x4x4 slice. The times are simulated.
128 devices in a mesh: row: 8 (over z_hi, x), sub: 16 (over z_lo, y, core).
Axes of the slice: x: 4, y: 4, z: 4 (z_hi: 2, z_lo: 2; z = z_hi * 2 + z_lo), core: 2. Of those that a mesh axis runs over, the one named last changes fastest.
Arguments:
- ritz_coefficients: bfloat16 [16384, 2048], P('row', 'sub'), may hold values from -6 to 6
- mode_map: int32 [128, 128], P(('row', 'sub')), may hold values from 0 to 127, each once within a row
- leaf_count: int32 [128], P(('row', 'sub')), may hold values from 24 to 48, as said below
- mode_blocks: bfloat16 [133120, 2048], P(('row', 'sub'))
Outputs:
- eigenvectors: bfloat16 [262144, 2048], P(('row', 'sub'))
Inputs may be any that keep to these rules, and one draw needn't show every extreme that they name: `mode_map`: each row is a permutation of 0 to 127. `leaf_count`: some substructure uses all 48 interior modes.
All inputs are finite; a program needn't handle non-finite values.
Results may differ from a plain program's by a relative error of at most 0.001.
Values may be sent and summed in bfloat16 or wider, within the bound.
No kernel may reach another device: no remote copies, remote signals or barrier semaphores. Data moves between devices by JAX's collectives and lax.ppermute only.
A program may use at most 64 MiB of HBM per device.

v0:
```python
import functools

import jax
import jax.numpy as jnp
from jax import lax
from jax.experimental import pallas as pl
from jax.experimental.pallas import tpu as pltpu
from jax.sharding import PartitionSpec as P


SR = 16
LEVELS = 5
AXES = ("row", "sub")


OWN = [(0, l) for l in (1, 2, 3, 4, 5)]
FIRST = (
    [(2, l) for l in (2, 3, 4, 5)]
    + [(6, l) for l in (3, 4, 5)]
    + [(4, l) for l in (3, 4, 5)]
    + [(8, l) for l in (4, 5)]
    + [(16, 5), (24, 5)]
)
SECOND = (
    [(10, 4), (10, 5), (26, 5)]
    + [(14, 4), (14, 5), (30, 5)]
    + [(12, 4), (12, 5)]
    + [(18, 5), (22, 5), (20, 5)]
    + [(28, 5)]
)


def partner(shares):
    return [(m ^ 1, l) for m, l in shares]


CHUNKS = (
    [None, None, None] + OWN + partner(OWN),
    FIRST + partner(FIRST),
    SECOND + partner(SECOND),
)


def exchange(value, mask):
    return lax.ppermute(value, AXES, [(i, i ^ mask) for i in range(128)])


def arrange_kernel(blocks, *refs):
    outs, rows, sem = refs[:-2], refs[-2], refs[-1]
    device = lax.axis_index("row") * lax.axis_size("sub") + lax.axis_index("sub")
    order = [share for chunk in CHUNKS for share in chunk]
    copies = []
    for slot, share in enumerate(order):
        if share is None:
            block = slot
        else:
            mask, level = share
            block = (1 << level) + 1 + ((device ^ mask) & ((1 << level) - 1))
        copies.append(
            pltpu.make_async_copy(
                blocks.at[pl.ds(pl.multiple_of(block * SR, SR), SR), :],
                rows.at[slot * SR : (slot + 1) * SR, :],
                sem,
            )
        )
    for copy in copies:
        copy.start()
    for copy in copies:
        copy.wait()
    at = 0
    for out in outs:
        depth = out.shape[1]
        out[...] = rows[at : at + depth, :].T
        at += depth


def arrange(blocks):
    ndof = blocks.shape[1]
    return pl.pallas_call(
        arrange_kernel,
        out_shape=[pltpu.VMEM((ndof, SR * len(c)), jnp.bfloat16) for c in CHUNKS],
        in_specs=[pl.BlockSpec(memory_space=pl.ANY)],
        out_specs=[pl.BlockSpec(memory_space=pltpu.VMEM)] * len(CHUNKS),
        scratch_shapes=[pltpu.VMEM(blocks.shape, jnp.bfloat16), pltpu.SemaphoreType.DMA],
        compiler_params=pltpu.CompilerParams(vmem_limit_bytes=GRANT),
        cost_estimate=pl.CostEstimate(flops=0, bytes_accessed=9 << 20, transcendentals=0),
        name="arrange",
    )(blocks)


TILE = 512
GRANT = 12 << 20
SMALL = 4 << 20


def product_kernel(first, last, count, modes, *refs):
    pieces, refs = refs[:count], refs[count:]
    if not first:
        total_in, refs = refs[0], refs[1:]
    if not last:
        total = refs[0]
    else:
        out, buf, sem = refs
    width = pieces[0].shape[1]
    steps = width // TILE

    def send(step):
        return pltpu.make_async_copy(
            buf.at[step % 2],
            out.at[:, pl.ds(pl.multiple_of(step * TILE, TILE), TILE)],
            sem.at[step % 2],
        )

    @pl.loop(0, steps)
    def _(step):
        columns = pl.ds(pl.multiple_of(step * TILE, TILE), TILE)
        value = jnp.dot(
            modes[...],
            jnp.concatenate([p[:, columns] for p in pieces], axis=0),
            preferred_element_type=jnp.float32,
        )
        if not first:
            value = value + total_in[:, columns]
        if not last:
            total[:, columns] = value
        else:

            @pl.when(step >= 2)
            def _():
                send(step - 2).wait()

            buf[step % 2] = value.astype(jnp.bfloat16)
            send(step).start()

    if last:
        send(steps - 2).wait()
        send(steps - 1).wait()


def product(modes, pieces, total=None, last=False):
    ndof, depth = modes.shape
    width = pieces[0].shape[1]
    first = total is None
    vmem = pl.BlockSpec(memory_space=pltpu.VMEM)
    operands = [modes, *pieces] + ([] if first else [total])
    if last:
        out_shape = jax.ShapeDtypeStruct((ndof, width), jnp.bfloat16)
        out_spec = pl.BlockSpec(memory_space=pl.ANY)
        scratch = [pltpu.VMEM((2, ndof, TILE), jnp.bfloat16), pltpu.SemaphoreType.DMA((2,))]
        alias = {}
    else:
        out_shape = pltpu.VMEM((ndof, width), jnp.float32)
        out_spec = vmem
        scratch = []
        alias = {} if first else {len(operands) - 1: 0}
    return pl.pallas_call(
        functools.partial(product_kernel, first, last, len(pieces)),
        out_shape=out_shape,
        in_specs=[vmem] * len(operands),
        out_specs=out_spec,
        scratch_shapes=scratch,
        input_output_aliases=alias,
        compiler_params=pltpu.CompilerParams(vmem_limit_bytes=GRANT),
        cost_estimate=pl.CostEstimate(
            flops=2 * ndof * width * depth, bytes_accessed=8 << 20, transcendentals=0
        ),
    )(*operands)


def place_kernel(leaf, count, slots, blocks, _, out):
    kept = out.shape[0]
    rows = lax.broadcasted_iota(jnp.int32, (kept, kept), 0)
    live = (rows >= leaf) | (rows < count[0])
    pick = jnp.where((rows == slots[...]) & live, 1.0, 0.0).astype(jnp.bfloat16)
    for part in range(blocks.shape[0]):
        columns = slice(part * blocks.shape[2], (part + 1) * blocks.shape[2])
        out[:, columns] = jnp.dot(
            pick, blocks[part], preferred_element_type=jnp.float32
        ).astype(jnp.bfloat16)


def place(mode_map, leaf_count, blocks, after):
    parts, kept, width = blocks.shape
    return pl.pallas_call(
        functools.partial(place_kernel, kept - LEVELS * SR),
        out_shape=pltpu.VMEM((kept, parts * width), jnp.bfloat16),
        in_specs=[
            pl.BlockSpec(memory_space=pltpu.SMEM),
            pl.BlockSpec(memory_space=pltpu.VMEM),
            pl.BlockSpec(memory_space=pltpu.VMEM),
            pl.BlockSpec(memory_space=pl.ANY),
        ],
        out_specs=pl.BlockSpec(memory_space=pltpu.VMEM),
        compiler_params=pltpu.CompilerParams(vmem_limit_bytes=SMALL),
        name="place",
    )(leaf_count, mode_map, blocks, after)


def pack_kernel(starts, count, *refs):
    out, at = refs[-1], 0
    for start, piece in zip(starts, refs[:count]):
        depth = piece.shape[0] - start
        out[at : at + depth, :] = piece[start:, :]
        at += depth


def pack(pieces, starts, *after):
    depth = sum(p.shape[0] - s for p, s in zip(pieces, starts))
    return pl.pallas_call(
        functools.partial(pack_kernel, starts, len(pieces)),
        out_shape=pltpu.VMEM((depth, pieces[0].shape[1]), jnp.bfloat16),
        in_specs=[pl.BlockSpec(memory_space=pltpu.VMEM)] * len(pieces)
        + [pl.BlockSpec(memory_space=pl.ANY)] * len(after),
        out_specs=pl.BlockSpec(memory_space=pltpu.VMEM),
        compiler_params=pltpu.CompilerParams(vmem_limit_bytes=SMALL),
    )(*pieces, *after)


def shards(ritz_coefficients, mode_map, leaf_count, mode_blocks):
    modes = arrange(mode_blocks)
    parts = lax.axis_size("sub")
    width = ritz_coefficients.shape[1]
    blocks = ritz_coefficients.reshape(parts, -1, width)
    blocks = lax.all_to_all(blocks, "sub", split_axis=0, concat_axis=0, tiled=True)
    coeffs = place(mode_map, leaf_count, blocks, modes[0])
    leaf = coeffs.shape[0] - LEVELS * SR

    def shares(low):
        return coeffs[leaf + (low - 1) * SR :]

    own = shares(1)
    h = exchange(shares(3), 4)
    f = exchange(shares(2), 2)
    g = exchange(shares(3), 6)
    z = exchange(shares(4), 8)
    x = exchange(shares(5), 16)
    xz = exchange(shares(5), 24)
    total = product(modes[0], [coeffs[:leaf], own, exchange(own, 1)])
    along_y = pack([z, xz], [0, 0], total)
    along_x = pack([f, g, h], [48, 32, 32], total)
    first = [f, g, h, z, x, xz]
    second = [
        exchange(along_y, 2),
        exchange(along_y, 6),
        exchange(h[16:], 8),
        exchange(along_x, 16),
        exchange(h[32:], 24),
    ]
    first += [exchange(p, 1) for p in first]
    total = product(modes[1], first, total)
    second += [exchange(p, 1) for p in second]
    return product(modes[2], second, total, last=True)


def solution(mesh):
    return jax.shard_map(
        shards,
        mesh=mesh,
        in_specs=(
            P("row", "sub"),
            P(("row", "sub"), None),
            P(("row", "sub")),
            P(("row", "sub"), None),
        ),
        out_specs=P(("row", "sub"), None),
        check_vma=False,
    )
```

profile of v0, /device:TPU:0, one launch (start us, length us, event | category | flops | bytes accessed | tf_op | source)
XLA Modules:
  0.0 71.3 jit_solution(17486325711279705975)
XLA Ops:
  0.0 6.1 %all-to-all-start = ((bf16[16,128,128]{2,1,0:T(8,128)(2,1)}), bf16[16,128,128]{2,1,0:T(8,128)(2,1)}, u32[]{:S(2)}, u32[]{:S(2)}) async-start(bf16[16,128,128]{2,1,0:T(8,128)(2,1)} %bitcast.1), calls=%async_computation | async-start | bytes 1048576 | tf_op jit(solution)/shard_map/all_to_all | solution.py:224
  6.1 0.0 copy-start
  6.1 2.2 %copy-done = bf16[1040,2048]{1,0:T(8,128)(2,1)S(1)} copy-done((bf16[1040,2048]{1,0:T(8,128)(2,1)S(1)}, bf16[1040,2048]{1,0:T(8,128)(2,1)}, u32[]{:S(2)}) %copy-start) | copy-done | bytes 4259864
  8.3 7.0 %arrange.1 = (bf16[2048,208]{1,0:T(8,128)(2,1)S(1)}, bf16[2048,448]{1,0:T(8,128)(2,1)S(1)}, bf16[2048,384]{1,0:T(8,128)(2,1)S(1)}) custom-call(bf16[1040,2048]{1,0:T(8,128)(2,1)S(1)} %copy-done), custom_call_target="tpu_custom_call" | custom-call | bytes 9437184 | tf_op jit(solution)/shard_map/arrange/pallas_call | solution.py:79
  15.3 0.0 copy-start.1
  15.3 1.1 %copy-done.1 = bf16[2048,384]{1,0:T(8,128)(2,1)} copy-done((bf16[2048,384]{1,0:T(8,128)(2,1)}, bf16[2048,384]{1,0:T(8,128)(2,1)S(1)}, u32[]{:S(2)}) %copy-start.1) | copy-done | bytes 1572888
  17.1 0.6 copy-done.3
  17.8 1.3 %place.1 = bf16[128,2048]{1,0:T(8,128)(2,1)S(1)} custom-call(s32[1]{0:T(128)S(6)} %copy.7.count, s32[1,128]{1,0:T(1,128)S(1)} %copy-done.3, bf16[16,128,128]{2,1,0:T(8,128)(2,1)} %all-to-all-done.blocks, bf16[2048,208]{1,0:T(8,128)(2,1)S(1)} %get-tuple-element.9._.modes), custom_call_target="tpu_custom_call" | custom-call | tf_op jit(solution)/shard_map/place/pallas_call | solution.py:184
  19.1 2.9 %collective-permute-start.1 = (bf16[16,2048]{1,0:T(8,128)(2,1)S(1)}, bf16[16,2048]{1,0:T(8,128)(2,1)S(1)}, u32[]{:S(2)}, u32[]{:S(2)}) collective-permute-start(bf16[16,2048]{1,0:T(8,128)(2,1)S(1)} %slice.35), channel_id=1, source_target_pairs={{0,24},{1,25},{2,26},{3,27},{4,28},{5,29},{6,30},{7,31},{8,16},{9,... | collective-permute-start | bytes 196616 | tf_op jit(solution)/shard_map/ppermute | solution.py:45
  22.0 0.6 collective-permute-start.16
  22.7 1.5 %collective-permute-start.7 = (bf16[64,2048]{1,0:T(8,128)(2,1)S(1)}, bf16[64,2048]{1,0:T(8,128)(2,1)S(1)}, u32[]{:S(2)}, u32[]{:S(2)}) collective-permute-start(bf16[64,2048]{1,0:T(8,128)(2,1)S(1)} %slice.40), channel_id=1, source_target_pairs={{0,2},{1,3},{2,0},{3,1},{4,6},{5,7},{6,4},{7,5},{8,10},{9,11},{10,... | collective-permute-start | bytes 786440 | tf_op jit(solution)/shard_map/ppermute | solution.py:45
  24.1 0.4 collective-permute-done.1.refs_1_.refs_5_
  24.5 3.5 %collective-permute-start.5 = (bf16[48,2048]{1,0:T(8,128)(2,1)S(1)}, bf16[48,2048]{1,0:T(8,128)(2,1)S(1)}, u32[]{:S(2)}, u32[]{:S(2)}) collective-permute-start(bf16[48,2048]{1,0:T(8,128)(2,1)S(1)} %get-tuple-element.11), channel_id=1, source_target_pairs={{0,4},{1,5},{2,6},{3,7},{4,0},{5,1},{6,2},{7,3},{8,12},{9,13},{10,... | collective-permute-start | bytes 589832 | tf_op jit(solution)/shard_map/ppermute | solution.py:45
  28.1 0.2 collective-permute-start.21
  28.3 1.2 %collective-permute-start.8 = (bf16[48,2048]{1,0:T(8,128)(2,1)S(1)}, bf16[48,2048]{1,0:T(8,128)(2,1)S(1)}, u32[]{:S(2)}, u32[]{:S(2)}) collective-permute-start(bf16[48,2048]{1,0:T(8,128)(2,1)S(1)} %get-tuple-element.11), channel_id=1, source_target_pairs={{0,6},{1,7},{2,4},{3,5},{4,2},{5,3},{6,0},{7,1},{8,14},{9,15},{10,... | collective-permute-start | bytes 589832 | tf_op jit(solution)/shard_map/ppermute | solution.py:45
  29.5 1.5 %collective-permute-start = (bf16[32,2048]{1,0:T(8,128)(2,1)S(1)}, bf16[32,2048]{1,0:T(8,128)(2,1)S(1)}, u32[]{:S(2)}, u32[]{:S(2)}) collective-permute-start(bf16[32,2048]{1,0:T(8,128)(2,1)S(1)} %slice.34), channel_id=1, source_target_pairs={{0,8},{1,9},{2,10},{3,11},{4,12},{5,13},{6,14},{7,15},{8,0},{9,1},... | collective-permute-start | bytes 393224 | tf_op jit(solution)/shard_map/ppermute | solution.py:45
  31.0 6.8 %collective-permute-done.5.refs_2_ = bf16[48,2048]{1,0:T(8,128)(2,1)S(1)} collective-permute-done((bf16[48,2048]{1,0:T(8,128)(2,1)S(1)}, bf16[48,2048]{1,0:T(8,128)(2,1)S(1)}, u32[]{:S(2)}, u32[]{:S(2)}) %collective-permute-start.5) | collective-permute-done | bytes 196640 | tf_op jit(solution)/shard_map/ppermute | solution.py:45
  37.9 0.6 collective-permute-start.20
  38.4 2.4 %collective-permute-done.8.refs_1_ = bf16[48,2048]{1,0:T(8,128)(2,1)S(1)} collective-permute-done((bf16[48,2048]{1,0:T(8,128)(2,1)S(1)}, bf16[48,2048]{1,0:T(8,128)(2,1)S(1)}, u32[]{:S(2)}, u32[]{:S(2)}) %collective-permute-start.8) | collective-permute-done | bytes 196640 | tf_op jit(solution)/shard_map/ppermute | solution.py:45
  40.8 1.3 %collective-permute-start.6 = (bf16[32,2048]{1,0:T(8,128)(2,1)S(1)}, bf16[32,2048]{1,0:T(8,128)(2,1)S(1)}, u32[]{:S(2)}, u32[]{:S(2)}) collective-permute-start(bf16[32,2048]{1,0:T(8,128)(2,1)S(1)} %slice.39), channel_id=1, source_target_pairs={{0,8},{1,9},{2,10},{3,11},{4,12},{5,13},{6,14},{7,15},{8,0},{9,1},... | collective-permute-start | bytes 393224 | tf_op jit(solution)/shard_map/ppermute | solution.py:45
  42.1 2.0 %collective-permute-start.10 = (bf16[16,2048]{1,0:T(8,128)(2,1)S(1)}, bf16[16,2048]{1,0:T(8,128)(2,1)S(1)}, u32[]{:S(2)}, u32[]{:S(2)}) collective-permute-start(bf16[16,2048]{1,0:T(8,128)(2,1)S(1)} %slice.41), channel_id=1, source_target_pairs={{0,24},{1,25},{2,26},{3,27},{4,28},{5,29},{6,30},{7,31},{8,16},{9,... | collective-permute-start | bytes 196616 | tf_op jit(solution)/shard_map/ppermute | solution.py:45
  44.1 2.8 %shard_map.46.refs_2_.refs_3_.refs_12_ = f32[2048,2048]{1,0:T(8,128)S(1)} custom-call(bf16[2048,208]{1,0:T(8,128)(2,1)S(1)} %get-tuple-element.9._.modes, bf16[48,2048]{1,0:T(8,128)(2,1)S(1)} %get-tuple-element.12.refs_0_, bf16[80,2048]{1,0:T(8,128)(2,1)S(1)} %slice.37.refs_1_, bf16[80,2048]{1,0:T(8,128)(2,1)S(1)} %collective-permute-done.2.refs_2_), custom_call_target="tpu_custom_call" | custom-call | flops 1744830464 | bytes 8388608 | tf_op jit(solution)/shard_map/pallas_call | solution.py:156
  47.0 0.3 collective-permute-done.10.refs_4_
  47.3 0.3 collective-permute-start.18
  47.6 1.5 %collective-permute-start.9 = (bf16[48,2048]{1,0:T(8,128)(2,1)S(1)}, bf16[48,2048]{1,0:T(8,128)(2,1)S(1)}, u32[]{:S(2)}, u32[]{:S(2)}) collective-permute-start(bf16[48,2048]{1,0:T(8,128)(2,1)S(1)} %shard_map.48), channel_id=1, source_target_pairs={{0,16},{1,17},{2,18},{3,19},{4,20},{5,21},{6,22},{7,23},{8,24},{9,... | collective-permute-start | bytes 589832 | tf_op jit(solution)/shard_map/ppermute | solution.py:45
  49.1 0.5 collective-permute-start.4
  49.5 5.1 %collective-permute-done.9.refs_3_ = bf16[48,2048]{1,0:T(8,128)(2,1)S(1)} collective-permute-done((bf16[48,2048]{1,0:T(8,128)(2,1)S(1)}, bf16[48,2048]{1,0:T(8,128)(2,1)S(1)}, u32[]{:S(2)}, u32[]{:S(2)}) %collective-permute-start.9) | collective-permute-done | bytes 196640 | tf_op jit(solution)/shard_map/ppermute | solution.py:45
  54.6 1.5 %collective-permute-done.3.refs_0_ = bf16[48,2048]{1,0:T(8,128)(2,1)S(1)} collective-permute-done((bf16[48,2048]{1,0:T(8,128)(2,1)S(1)}, bf16[48,2048]{1,0:T(8,128)(2,1)S(1)}, u32[]{:S(2)}, u32[]{:S(2)}) %collective-permute-start.3) | collective-permute-done | bytes 196640 | tf_op jit(solution)/shard_map/ppermute | solution.py:45
  56.1 1.3 %collective-permute-done.4.refs_1_ = bf16[48,2048]{1,0:T(8,128)(2,1)S(1)} collective-permute-done((bf16[48,2048]{1,0:T(8,128)(2,1)S(1)}, bf16[48,2048]{1,0:T(8,128)(2,1)S(1)}, u32[]{:S(2)}, u32[]{:S(2)}) %collective-permute-start.4) | collective-permute-done | bytes 196640 | tf_op jit(solution)/shard_map/ppermute | solution.py:45
  57.4 0.5 collective-permute-start.12
  57.9 6.2 %shard_map.49.refs_10_ = f32[2048,2048]{1,0:T(8,128)S(1)} custom-call(bf16[2048,448]{1,0:T(8,128)(2,1)S(1)} %get-tuple-element.10.modes, bf16[64,2048]{1,0:T(8,128)(2,1)S(1)} %collective-permute-done.7.refs_0_, bf16[48,2048]{1,0:T(8,128)(2,1)S(1)} %collective-permute-done.8.refs_1_, ...), custom_call_target="tpu_custom_call", output_to_operand_aliasing={{}: (13, {})} | custom-call | flops 3758096384 | bytes 8388608 | tf_op jit(solution)/shard_map/pallas_call | solution.py:156
  64.2 7.2 %shard_map.50 = bf16[2048,2048]{1,0:T(8,128)(2,1)} custom-call(bf16[2048,384]{1,0:T(8,128)(2,1)S(1)} %copy-done.2, bf16[48,2048]{1,0:T(8,128)(2,1)S(1)} %collective-permute-done.3.refs_0_, bf16[48,2048]{1,0:T(8,128)(2,1)S(1)} %collective-permute-done.4.refs_1_, bf16[32,2048]{1,0:T(8,128)(2,1)S(1)} %collective-permute-done.6.refs_2_, ...), custom_call_target="tpu_custom_call" | custom-call | flops 3221225472 | bytes 8388608 | tf_op jit(solution)/shard_map/pallas_call | solution.py:156
  (38 shorter events, 0.2 us)
Async XLA Ops:
  0.0 17.1 %all-to-all-start = ((bf16[16,128,128]{2,1,0:T(8,128)(2,1)}), bf16[16,128,128]{2,1,0:T(8,128)(2,1)}, u32[]{:S(2)}, u32[]{:S(2)}) async-start(bf16[16,128,128]{2,1,0:T(8,128)(2,1)} %bitcast.1), calls=%async_computation | async-start | bytes 1048576 | tf_op jit(solution)/shard_map/all_to_all | solution.py:224
  6.1 2.2 %copy-start = (bf16[1040,2048]{1,0:T(8,128)(2,1)S(1)}, bf16[1040,2048]{1,0:T(8,128)(2,1)}, u32[]{:S(2)}) copy-start(bf16[1040,2048]{1,0:T(8,128)(2,1)} %blocks.1) | copy-start | bytes 12779524
  15.3 1.1 %copy-start.1 = (bf16[2048,384]{1,0:T(8,128)(2,1)}, bf16[2048,384]{1,0:T(8,128)(2,1)S(1)}, u32[]{:S(2)}) copy-start(bf16[2048,384]{1,0:T(8,128)(2,1)S(1)} %get-tuple-element.8.modes) | copy-start | bytes 4718596
  17.1 0.7 copy-start.3
  19.1 5.4 %collective-permute-start.1 = (bf16[16,2048]{1,0:T(8,128)(2,1)S(1)}, bf16[16,2048]{1,0:T(8,128)(2,1)S(1)}, u32[]{:S(2)}, u32[]{:S(2)}) collective-permute-start(bf16[16,2048]{1,0:T(8,128)(2,1)S(1)} %slice.35), channel_id=1, source_target_pairs={{0,24},{1,25},{2,26},{3,27},{4,28},{5,29},{6,30},{7,31},{8,16},{9,... | collective-permute-start | bytes 196616 | tf_op jit(solution)/shard_map/ppermute | solution.py:45
  22.0 6.0 %collective-permute-start.16 = (bf16[16,2048]{1,0:T(8,128)(2,1)S(1)}, bf16[16,2048]{1,0:T(8,128)(2,1)S(1)}, u32[]{:S(2)}, u32[]{:S(2)}) collective-permute-start(bf16[16,2048]{1,0:T(8,128)(2,1)S(1)} %slice.35), channel_id=1, source_target_pairs={{0,16},{1,17},{2,18},{3,19},{4,20},{5,21},{6,22},{7,23},{8,24},{9,... | collective-permute-start | bytes 196616 | tf_op jit(solution)/shard_map/ppermute | solution.py:45
  22.7 21.4 %collective-permute-start.2 = (bf16[80,2048]{1,0:T(8,128)(2,1)S(1)}, bf16[80,2048]{1,0:T(8,128)(2,1)S(1)}, u32[]{:S(2)}, u32[]{:S(2)}) collective-permute-start(bf16[80,2048]{1,0:T(8,128)(2,1)S(1)} %slice.37.refs_1_), channel_id=1, source_target_pairs={{0,1},{1,0},{2,3},{3,2},{4,5},{5,4},{6,7},{7,6},{8,9},{9,8},{10,11... | collective-permute-start | bytes 983048 | tf_op jit(solution)/shard_map/ppermute | solution.py:45
  22.7 19.5 %collective-permute-start.7 = (bf16[64,2048]{1,0:T(8,128)(2,1)S(1)}, bf16[64,2048]{1,0:T(8,128)(2,1)S(1)}, u32[]{:S(2)}, u32[]{:S(2)}) collective-permute-start(bf16[64,2048]{1,0:T(8,128)(2,1)S(1)} %slice.40), channel_id=1, source_target_pairs={{0,2},{1,3},{2,0},{3,1},{4,6},{5,7},{6,4},{7,5},{8,10},{9,11},{10,... | collective-permute-start | bytes 786440 | tf_op jit(solution)/shard_map/ppermute | solution.py:45
  24.5 3.8 %collective-permute-start.22 = (bf16[16,2048]{1,0:T(8,128)(2,1)S(1)}, bf16[16,2048]{1,0:T(8,128)(2,1)S(1)}, u32[]{:S(2)}, u32[]{:S(2)}) collective-permute-start(bf16[16,2048]{1,0:T(8,128)(2,1)S(1)} %collective-permute-done.1.refs_1_.refs_5_), channel_id=1, source_target_pairs={{0,1},{1,0},{2,3},{3,2},{4,5},{5,4},{6,7},{7,6},{8,9},{9,8},{10,11... | collective-permute-start | bytes 196616 | tf_op jit(solution)/shard_map/ppermute | solution.py:45
  24.5 13.3 %collective-permute-start.5 = (bf16[48,2048]{1,0:T(8,128)(2,1)S(1)}, bf16[48,2048]{1,0:T(8,128)(2,1)S(1)}, u32[]{:S(2)}, u32[]{:S(2)}) collective-permute-start(bf16[48,2048]{1,0:T(8,128)(2,1)S(1)} %get-tuple-element.11), channel_id=1, source_target_pairs={{0,4},{1,5},{2,6},{3,7},{4,0},{5,1},{6,2},{7,3},{8,12},{9,13},{10,... | collective-permute-start | bytes 589832 | tf_op jit(solution)/shard_map/ppermute | solution.py:45
  28.1 1.4 %collective-permute-start.21 = (bf16[16,2048]{1,0:T(8,128)(2,1)S(1)}, bf16[16,2048]{1,0:T(8,128)(2,1)S(1)}, u32[]{:S(2)}, u32[]{:S(2)}) collective-permute-start(bf16[16,2048]{1,0:T(8,128)(2,1)S(1)} %collective-permute-done.16.refs_4_), channel_id=1, source_target_pairs={{0,1},{1,0},{2,3},{3,2},{4,5},{5,4},{6,7},{7,6},{8,9},{9,8},{10,11... | collective-permute-start | bytes 196616 | tf_op jit(solution)/shard_map/ppermute | solution.py:45
  28.3 12.5 %collective-permute-start.8 = (bf16[48,2048]{1,0:T(8,128)(2,1)S(1)}, bf16[48,2048]{1,0:T(8,128)(2,1)S(1)}, u32[]{:S(2)}, u32[]{:S(2)}) collective-permute-start(bf16[48,2048]{1,0:T(8,128)(2,1)S(1)} %get-tuple-element.11), channel_id=1, source_target_pairs={{0,6},{1,7},{2,4},{3,5},{4,2},{5,3},{6,0},{7,1},{8,14},{9,15},{10,... | collective-permute-start | bytes 589832 | tf_op jit(solution)/shard_map/ppermute | solution.py:45
  29.5 8.4 %collective-permute-start = (bf16[32,2048]{1,0:T(8,128)(2,1)S(1)}, bf16[32,2048]{1,0:T(8,128)(2,1)S(1)}, u32[]{:S(2)}, u32[]{:S(2)}) collective-permute-start(bf16[32,2048]{1,0:T(8,128)(2,1)S(1)} %slice.34), channel_id=1, source_target_pairs={{0,8},{1,9},{2,10},{3,11},{4,12},{5,13},{6,14},{7,15},{8,0},{9,1},... | collective-permute-start | bytes 393224 | tf_op jit(solution)/shard_map/ppermute | solution.py:45
  37.8 11.3 %collective-permute-start.19 = (bf16[48,2048]{1,0:T(8,128)(2,1)S(1)}, bf16[48,2048]{1,0:T(8,128)(2,1)S(1)}, u32[]{:S(2)}, u32[]{:S(2)}) collective-permute-start(bf16[48,2048]{1,0:T(8,128)(2,1)S(1)} %collective-permute-done.5.refs_2_), channel_id=1, source_target_pairs={{0,1},{1,0},{2,3},{3,2},{4,5},{5,4},{6,7},{7,6},{8,9},{9,8},{10,11... | collective-permute-start | bytes 589832 | tf_op jit(solution)/shard_map/ppermute | solution.py:45
  37.9 9.7 %collective-permute-start.20 = (bf16[32,2048]{1,0:T(8,128)(2,1)S(1)}, bf16[32,2048]{1,0:T(8,128)(2,1)S(1)}, u32[]{:S(2)}, u32[]{:S(2)}) collective-permute-start(bf16[32,2048]{1,0:T(8,128)(2,1)S(1)} %collective-permute-done.refs_0_.refs_3_), channel_id=1, source_target_pairs={{0,1},{1,0},{2,3},{3,2},{4,5},{5,4},{6,7},{7,6},{8,9},{9,8},{10,11... | collective-permute-start | bytes 393224 | tf_op jit(solution)/shard_map/ppermute | solution.py:45
  40.8 8.3 %collective-permute-start.6 = (bf16[32,2048]{1,0:T(8,128)(2,1)S(1)}, bf16[32,2048]{1,0:T(8,128)(2,1)S(1)}, u32[]{:S(2)}, u32[]{:S(2)}) collective-permute-start(bf16[32,2048]{1,0:T(8,128)(2,1)S(1)} %slice.39), channel_id=1, source_target_pairs={{0,8},{1,9},{2,10},{3,11},{4,12},{5,13},{6,14},{7,15},{8,0},{9,1},... | collective-permute-start | bytes 393224 | tf_op jit(solution)/shard_map/ppermute | solution.py:45
  42.1 5.2 %collective-permute-start.10 = (bf16[16,2048]{1,0:T(8,128)(2,1)S(1)}, bf16[16,2048]{1,0:T(8,128)(2,1)S(1)}, u32[]{:S(2)}, u32[]{:S(2)}) collective-permute-start(bf16[16,2048]{1,0:T(8,128)(2,1)S(1)} %slice.41), channel_id=1, source_target_pairs={{0,24},{1,25},{2,26},{3,27},{4,28},{5,29},{6,30},{7,31},{8,16},{9,... | collective-permute-start | bytes 196616 | tf_op jit(solution)/shard_map/ppermute | solution.py:45
  44.1 13.3 %collective-permute-start.17 = (bf16[64,2048]{1,0:T(8,128)(2,1)S(1)}, bf16[64,2048]{1,0:T(8,128)(2,1)S(1)}, u32[]{:S(2)}, u32[]{:S(2)}) collective-permute-start(bf16[64,2048]{1,0:T(8,128)(2,1)S(1)} %collective-permute-done.7.refs_0_), channel_id=1, source_target_pairs={{0,1},{1,0},{2,3},{3,2},{4,5},{5,4},{6,7},{7,6},{8,9},{9,8},{10,11... | collective-permute-start | bytes 786440 | tf_op jit(solution)/shard_map/ppermute | solution.py:45
  47.3 2.2 %collective-permute-start.18 = (bf16[48,2048]{1,0:T(8,128)(2,1)S(1)}, bf16[48,2048]{1,0:T(8,128)(2,1)S(1)}, u32[]{:S(2)}, u32[]{:S(2)}) collective-permute-start(bf16[48,2048]{1,0:T(8,128)(2,1)S(1)} %collective-permute-done.8.refs_1_), channel_id=1, source_target_pairs={{0,1},{1,0},{2,3},{3,2},{4,5},{5,4},{6,7},{7,6},{8,9},{9,8},{10,11... | collective-permute-start | bytes 589832 | tf_op jit(solution)/shard_map/ppermute | solution.py:45
  47.6 7.1 %collective-permute-start.9 = (bf16[48,2048]{1,0:T(8,128)(2,1)S(1)}, bf16[48,2048]{1,0:T(8,128)(2,1)S(1)}, u32[]{:S(2)}, u32[]{:S(2)}) collective-permute-start(bf16[48,2048]{1,0:T(8,128)(2,1)S(1)} %shard_map.48), channel_id=1, source_target_pairs={{0,16},{1,17},{2,18},{3,19},{4,20},{5,21},{6,22},{7,23},{8,24},{9,... | collective-permute-start | bytes 589832 | tf_op jit(solution)/shard_map/ppermute | solution.py:45
  49.1 7.0 %collective-permute-start.3 = (bf16[48,2048]{1,0:T(8,128)(2,1)S(1)}, bf16[48,2048]{1,0:T(8,128)(2,1)S(1)}, u32[]{:S(2)}, u32[]{:S(2)}) collective-permute-start(bf16[48,2048]{1,0:T(8,128)(2,1)S(1)} %shard_map.47), channel_id=1, source_target_pairs={{0,2},{1,3},{2,0},{3,1},{4,6},{5,7},{6,4},{7,5},{8,10},{9,11},{10,... | collective-permute-start | bytes 589832 | tf_op jit(solution)/shard_map/ppermute | solution.py:45
  49.1 8.3 %collective-permute-start.4 = (bf16[48,2048]{1,0:T(8,128)(2,1)S(1)}, bf16[48,2048]{1,0:T(8,128)(2,1)S(1)}, u32[]{:S(2)}, u32[]{:S(2)}) collective-permute-start(bf16[48,2048]{1,0:T(8,128)(2,1)S(1)} %shard_map.47), channel_id=1, source_target_pairs={{0,6},{1,7},{2,4},{3,5},{4,2},{5,3},{6,0},{7,1},{8,14},{9,15},{10,... | collective-permute-start | bytes 589832 | tf_op jit(solution)/shard_map/ppermute | solution.py:45
  49.5 14.6 %collective-permute-start.15 = (bf16[16,2048]{1,0:T(8,128)(2,1)S(1)}, bf16[16,2048]{1,0:T(8,128)(2,1)S(1)}, u32[]{:S(2)}, u32[]{:S(2)}) collective-permute-start(bf16[16,2048]{1,0:T(8,128)(2,1)S(1)} %collective-permute-done.10.refs_4_), channel_id=1, source_target_pairs={{0,1},{1,0},{2,3},{3,2},{4,5},{5,4},{6,7},{7,6},{8,9},{9,8},{10,11... | collective-permute-start | bytes 196616 | tf_op jit(solution)/shard_map/ppermute | solution.py:45
  54.6 9.5 %collective-permute-start.13 = (bf16[32,2048]{1,0:T(8,128)(2,1)S(1)}, bf16[32,2048]{1,0:T(8,128)(2,1)S(1)}, u32[]{:S(2)}, u32[]{:S(2)}) collective-permute-start(bf16[32,2048]{1,0:T(8,128)(2,1)S(1)} %collective-permute-done.6.refs_2_), channel_id=1, source_target_pairs={{0,1},{1,0},{2,3},{3,2},{4,5},{5,4},{6,7},{7,6},{8,9},{9,8},{10,11... | collective-permute-start | bytes 393224 | tf_op jit(solution)/shard_map/ppermute | solution.py:45
  56.1 8.0 %collective-permute-start.14 = (bf16[48,2048]{1,0:T(8,128)(2,1)S(1)}, bf16[48,2048]{1,0:T(8,128)(2,1)S(1)}, u32[]{:S(2)}, u32[]{:S(2)}) collective-permute-start(bf16[48,2048]{1,0:T(8,128)(2,1)S(1)} %collective-permute-done.9.refs_3_), channel_id=1, source_target_pairs={{0,1},{1,0},{2,3},{3,2},{4,5},{5,4},{6,7},{7,6},{8,9},{9,8},{10,11... | collective-permute-start | bytes 589832 | tf_op jit(solution)/shard_map/ppermute | solution.py:45
  57.4 6.7 %collective-permute-start.11 = (bf16[48,2048]{1,0:T(8,128)(2,1)S(1)}, bf16[48,2048]{1,0:T(8,128)(2,1)S(1)}, u32[]{:S(2)}, u32[]{:S(2)}) collective-permute-start(bf16[48,2048]{1,0:T(8,128)(2,1)S(1)} %collective-permute-done.3.refs_0_), channel_id=1, source_target_pairs={{0,1},{1,0},{2,3},{3,2},{4,5},{5,4},{6,7},{7,6},{8,9},{9,8},{10,11... | collective-permute-start | bytes 589832 | tf_op jit(solution)/shard_map/ppermute | solution.py:45
  57.4 6.7 %collective-permute-start.12 = (bf16[48,2048]{1,0:T(8,128)(2,1)S(1)}, bf16[48,2048]{1,0:T(8,128)(2,1)S(1)}, u32[]{:S(2)}, u32[]{:S(2)}) collective-permute-start(bf16[48,2048]{1,0:T(8,128)(2,1)S(1)} %collective-permute-done.4.refs_1_), channel_id=1, source_target_pairs={{0,1},{1,0},{2,3},{3,2},{4,5},{5,4},{6,7},{7,6},{8,9},{9,8},{10,11... | collective-permute-start | bytes 589832 | tf_op jit(solution)/shard_map/ppermute | solution.py:45
  57.9 6.2 %copy-start.2 = (bf16[2048,384]{1,0:T(8,128)(2,1)S(1)}, bf16[2048,384]{1,0:T(8,128)(2,1)}, u32[]{:S(2)}) copy-start(bf16[2048,384]{1,0:T(8,128)(2,1)} %copy-done.1) | copy-start | bytes 4718596
where the time goes:
time: 72.5 us; the launch traced here: 71.3 us
  Pallas kernels  24.5 us (34%)
  starting transfers between devices  24.1 us (33%)
  waiting for transfers between devices  17.7 us (24%)
  local copies, waits for them, and re-layouts  4.09 us (6%)
  between operations  0.86 us (1%)
    ppermute x23, starting transfers between devices, exchange(): return lax.ppermute(value, AXES, [(i, i ^ mask) for i in range(128)])  18 us
    ppermute x23, waiting for transfers between devices, exchange(): return lax.ppermute(value, AXES, [(i, i ^ mask) for i in range(128)])  17.7 us
    pallas_call x3, Pallas kernels, product(): pl.pallas_call(functools.partial(product_kernel, first, last, len(pieces)...  16.2 us
    pallas_call x1, Pallas kernels, arrange(): pl.pallas_call(arrange_kernel, out_shape=[pltpu.VMEM((ndof, SR * len(c)),...  6.97 us
    all_to_all x1, starting transfers between devices, shards(): lax.all_to_all(blocks, 'sub', split_axis=0, concat_axis=0, tiled=True)  6.09 us
    unnamed x8, local copies, waits for them, and re-layouts  3.99 us
  transfers between devices with their start and end apart: 24, of which 7 were waited for; matrix products, arithmetic and copies ran while one was open for 0% of the time, Pallas kernels for 22%

commit v1 on v0

v1 whole, which is shorter than its diff:
```python
import functools

import jax
import jax.numpy as jnp
from jax import lax
from jax.experimental import pallas as pl
from jax.experimental.pallas import tpu as pltpu
from jax.sharding import PartitionSpec as P


SR = 16
LEVELS = 5
AXES = ("row", "sub")


OWN = [(0, l) for l in (1, 2, 3, 4, 5)]
FIRST = (
    [(2, l) for l in (2, 3, 4, 5)]
    + [(6, l) for l in (3, 4, 5)]
    + [(4, l) for l in (3, 4, 5)]
    + [(8, l) for l in (4, 5)]
    + [(16, 5), (24, 5)]
)
SECOND = (
    [(10, 4), (10, 5), (26, 5)]
    + [(14, 4), (14, 5), (30, 5)]
    + [(12, 4), (12, 5)]
    + [(18, 5), (22, 5), (20, 5)]
    + [(28, 5)]
)


def partner(shares):
    return [(m ^ 1, l) for m, l in shares]


CHUNKS = (
    [None, None, None] + OWN + partner(OWN),
    FIRST + partner(FIRST),
    SECOND + partner(SECOND),
)


def exchange(value, mask):
    return lax.ppermute(value, AXES, [(i, i ^ mask) for i in range(128)])


def arrange_kernel(leaf, count, slots, blocks, *refs):
    outs, pick, rows, sem = refs[:-3], refs[-3], refs[-2], refs[-1]
    device = lax.axis_index("row") * lax.axis_size("sub") + lax.axis_index("sub")
    slot, waits = 0, []
    for number, chunk in enumerate(CHUNKS):
        copies = []
        for share in chunk:
            if share is None:
                block = slot
            else:
                mask, level = share
                block = (1 << level) + 1 + ((device ^ mask) & ((1 << level) - 1))
            copies.append(
                pltpu.make_async_copy(
                    blocks.at[pl.ds(pl.multiple_of(block * SR, SR), SR), :],
                    rows.at[slot * SR : (slot + 1) * SR, :],
                    sem.at[number],
                )
            )
            slot += 1
        for copy in copies:
            copy.start()
        waits.append(copies)
    local = lax.broadcasted_iota(jnp.int32, pick.shape, 0)
    live = (local >= leaf) | (local < count[0])
    pick[...] = jnp.where((local == slots[...]) & live, 1.0, 0.0).astype(jnp.bfloat16)
    at = 0
    for number, copies in enumerate(waits):
        for copy in copies:
            copy.wait()
        depth = SR * len(copies)
        outs[number][...] = rows[at : at + depth, :].T
        at += depth


def arrange(leaf_count, mode_map, blocks):
    ndof = blocks.shape[1]
    kept = mode_map.shape[1]
    vmem = pl.BlockSpec(memory_space=pltpu.VMEM)
    return pl.pallas_call(
        functools.partial(arrange_kernel, kept - LEVELS * SR),
        out_shape=[pltpu.VMEM((ndof, SR * len(c)), jnp.bfloat16) for c in CHUNKS]
        + [pltpu.VMEM((kept, kept), jnp.bfloat16)],
        in_specs=[
            pl.BlockSpec(memory_space=pltpu.SMEM),
            vmem,
            pl.BlockSpec(memory_space=pltpu.HBM),
        ],
        out_specs=[vmem] * (len(CHUNKS) + 1),
        scratch_shapes=[
            pltpu.VMEM(blocks.shape, jnp.bfloat16),
            pltpu.SemaphoreType.DMA((len(CHUNKS),)),
        ],
        compiler_params=pltpu.CompilerParams(vmem_limit_bytes=GRANT),
        cost_estimate=pl.CostEstimate(flops=0, bytes_accessed=9 << 20, transcendentals=0),
        name="arrange",
    )(leaf_count, mode_map, pltpu.with_memory_space_constraint(blocks, pltpu.HBM))


GRANT = 20 << 20
SMALL = 4 << 20


def product_kernel(first, last, tiles, count, modes, *refs):
    pieces, refs = refs[:count], refs[count:]
    if not first:
        total_in, refs = refs[0], refs[1:]
    if last:
        out, buf, sem = refs
    else:
        total = refs[0]
    sends = []
    for number, (at, height) in enumerate(tiles):
        rows = slice(at, at + height)
        value = jnp.dot(
            modes[rows, :],
            jnp.concatenate([p[...] for p in pieces], axis=0),
            preferred_element_type=jnp.float32,
        )
        if not first:
            value = value + total_in[rows, :]
        if last:
            buf[rows, :] = value.astype(jnp.bfloat16)
            sends.append(pltpu.make_async_copy(buf.at[rows, :], out.at[rows, :], sem.at[number]))
            sends[-1].start()
        else:
            total[rows, :] = value
    for send in sends:
        send.wait()


def product(number, modes, pieces, total=None, last=False):
    ndof = modes[number].shape[0]
    depth = SR * len(CHUNKS[number])
    width = pieces[0].shape[1]
    first = total is None
    vmem = pl.BlockSpec(memory_space=pltpu.VMEM)
    operands = [modes[number], *pieces] + ([] if first else [total])
    heights = LAST_TILES if last else TILES
    tiles, at = [], 0
    for height in heights:
        tiles.append((at, height))
        at += height
    if last:
        out_shape = jax.ShapeDtypeStruct((ndof, width), jnp.bfloat16)
        out_spec = pl.BlockSpec(memory_space=pl.ANY)
        scratch = [pltpu.VMEM((ndof, width), jnp.bfloat16), pltpu.SemaphoreType.DMA((len(tiles),))]
        alias = {}
    else:
        out_shape = pltpu.VMEM((ndof, width), jnp.float32)
        out_spec = vmem
        scratch = []
        alias = {} if first else {len(operands) - 1: 0}
    return pl.pallas_call(
        functools.partial(product_kernel, first, last, tiles, len(pieces)),
        out_shape=out_shape,
        in_specs=[vmem] * len(operands),
        out_specs=out_spec,
        scratch_shapes=scratch,
        input_output_aliases=alias,
        compiler_params=pltpu.CompilerParams(vmem_limit_bytes=GRANT),
        cost_estimate=pl.CostEstimate(
            flops=2 * ndof * width * depth, bytes_accessed=8 << 20, transcendentals=0
        ),
    )(*operands)


TILES = (1024, 1024)
LAST_TILES = (1024, 768, 256)


def place_kernel(pick, blocks, _, out):
    for part in range(blocks.shape[0]):
        columns = slice(part * blocks.shape[2], (part + 1) * blocks.shape[2])
        out[:, columns] = jnp.dot(
            pick[...], blocks[part], preferred_element_type=jnp.float32
        ).astype(jnp.bfloat16)


def place(pick, blocks, after):
    parts, kept, width = blocks.shape
    vmem = pl.BlockSpec(memory_space=pltpu.VMEM)
    return pl.pallas_call(
        place_kernel,
        out_shape=pltpu.VMEM((kept, parts * width), jnp.bfloat16),
        in_specs=[vmem, vmem, pl.BlockSpec(memory_space=pl.ANY)],
        out_specs=vmem,
        compiler_params=pltpu.CompilerParams(vmem_limit_bytes=SMALL),
        name="place",
    )(pick, blocks, after)


def pack_kernel(starts, *refs):
    out, at = refs[-1], 0
    for start, piece in zip(starts, refs):
        depth = piece.shape[0] - start
        out[at : at + depth, :] = piece[start:, :]
        at += depth


def pack(pieces, starts):
    depth = sum(p.shape[0] - s for p, s in zip(pieces, starts))
    return pl.pallas_call(
        functools.partial(pack_kernel, starts),
        out_shape=pltpu.VMEM((depth, pieces[0].shape[1]), jnp.bfloat16),
        in_specs=[pl.BlockSpec(memory_space=pltpu.VMEM)] * len(pieces),
        out_specs=pl.BlockSpec(memory_space=pltpu.VMEM),
        compiler_params=pltpu.CompilerParams(vmem_limit_bytes=SMALL),
    )(*pieces)


def shards(ritz_coefficients, mode_map, leaf_count, mode_blocks):
    *modes, pick = arrange(leaf_count, mode_map, mode_blocks)
    parts = lax.axis_size("sub")
    width = ritz_coefficients.shape[1]
    blocks = ritz_coefficients.reshape(parts, -1, width)
    blocks = lax.all_to_all(blocks, "sub", split_axis=0, concat_axis=0, tiled=True)
    coeffs = place(pick, blocks, modes[0])
    leaf = coeffs.shape[0] - LEVELS * SR

    def shares(low):
        return coeffs[leaf + (low - 1) * SR :]

    own = shares(1)
    h = exchange(shares(3), 4)
    f = exchange(shares(2), 2)
    g = exchange(shares(3), 6)
    z = exchange(shares(4), 8)
    x = exchange(shares(5), 16)
    xz = exchange(shares(5), 24)
    total = product(0, modes, [coeffs[:leaf], own, exchange(own, 1)])
    along_y = pack([z, xz], [0, 0])
    along_x = pack([f, g, h], [48, 32, 32])
    first = [f, g, h, z, x, xz]
    second = [
        exchange(along_y, 2),
        exchange(along_y, 6),
        exchange(h[16:], 8),
        exchange(along_x, 16),
        exchange(h[32:], 24),
    ]
    first += [exchange(p, 1) for p in first]
    total = product(1, modes, first, total)
    second += [exchange(p, 1) for p in second]
    return product(2, modes, second, total, last=True)


def solution(mesh):
    return jax.shard_map(
        shards,
        mesh=mesh,
        in_specs=(
            P("row", "sub"),
            P(("row", "sub"), None),
            P(("row", "sub")),
            P(("row", "sub"), None),
        ),
        out_specs=P(("row", "sub"), None),
        check_vma=False,
    )
```

time: 72.5 us -> 62 us (0.86)
  Pallas kernels: 24.5 us -> 17.7 us
  local copies, waits for them, and re-layouts: 4.09 us -> 1.89 us
  waiting for transfers between devices: 17.7 us -> 16.3 us
    ppermute x23, waiting for transfers between devices: 17.7 us -> 10.7 us  [exchange(): return lax.ppermute(value, AXES, [(i, i ^ mask) for i in range(128)])]
    pallas_call x7, Pallas kernels: 24.5 us -> 17.7 us  [the longest x3 13.5 us: product(): pl.pallas_call(functools.partial(product_kernel, first, last, tiles, len(...]
    all_to_all x1, waiting for transfers between devices: 0.01 us -> 5.59 us  [shards(): lax.all_to_all(blocks, 'sub', split_axis=0, concat_axis=0, tiled=True)]
    unnamed x8 -> x6, local copies, waits for them, and re-layouts: 3.99 us -> 1.79 us
  transfers between devices with their start and end apart: 24 -> 24, of which waited for: 7 -> 7; matrix products, arithmetic and copies ran while one was open for 0% -> 0% of each run, Pallas kernels for 22% -> 17%
where the time goes in v1:
time: 62 us; the launch traced here: 60.9 us
  starting transfers between devices  24 us (39%)
  Pallas kernels  17.7 us (29%)
  waiting for transfers between devices  16.3 us (26%)
  local copies, waits for them, and re-layouts  1.89 us (3%)
  between operations  1 us (2%)
    ppermute x23, starting transfers between devices, exchange(): return lax.ppermute(value, AXES, [(i, i ^ mask) for i in range(128)])  17.9 us
    pallas_call x3, Pallas kernels, product(): pl.pallas_call(functools.partial(product_kernel, first, last, tiles, len(...  13.5 us
    ppermute x23, waiting for transfers between devices, exchange(): return lax.ppermute(value, AXES, [(i, i ^ mask) for i in range(128)])  10.7 us
    all_to_all x1, starting transfers between devices, shards(): lax.all_to_all(blocks, 'sub', split_axis=0, concat_axis=0, tiled=True)  6.09 us
    all_to_all x1, waiting for transfers between devices, shards(): lax.all_to_all(blocks, 'sub', split_axis=0, concat_axis=0, tiled=True)  5.59 us
    pallas_call x1, Pallas kernels, arrange(): pl.pallas_call(functools.partial(arrange_kernel, kept - LEVELS * SR), out...  2.83 us
    unnamed x6, local copies, waits for them, and re-layouts  1.79 us
    pallas_call x1, Pallas kernels, place(): pl.pallas_call(place_kernel, out_shape=pltpu.VMEM((kept, parts * width),...  1.33 us
  transfers between devices with their start and end apart: 24, of which 7 were waited for; matrix products, arithmetic and copies ran while one was open for 0% of the time, Pallas kernels for 17%

profile of v1, /device:TPU:0, one launch (start us, length us, event | category | flops | bytes accessed | tf_op | source)
XLA Modules:
  0.0 60.9 jit_solution(342981085423313300)
XLA Ops:
  0.0 6.1 %all-to-all-start = ((bf16[16,128,128]{2,1,0:T(8,128)(2,1)}), bf16[16,128,128]{2,1,0:T(8,128)(2,1)}, u32[]{:S(2)}, u32[]{:S(2)}) async-start(bf16[16,128,128]{2,1,0:T(8,128)(2,1)} %bitcast.1), calls=%async_computation | async-start | bytes 1048576 | tf_op jit(solution)/shard_map/all_to_all | solution.py:224
  6.8 0.6 %copy-done.2 = s32[1,128]{1,0:T(1,128)S(1)} copy-done((s32[1,128]{1,0:T(1,128)S(1)}, s32[1,128]{1,0:T(1,128)}, u32[]{:S(2)}) %copy-start.2) | copy-done | bytes 536
  7.4 2.8 %arrange.1 = (bf16[2048,208]{1,0:T(8,128)(2,1)S(1)}, bf16[2048,448]{1,0:T(8,128)(2,1)S(1)}, bf16[2048,384]{1,0:T(8,128)(2,1)S(1)}, bf16[128,128]{1,0:T(8,128)(2,1)S(1)}) custom-call(s32[1]{0:T(128)S(6)} %copy.7.count, s32[1,128]{1,0:T(1,128)S(1)} %copy-done.2, bf16[1040,2048]{1,0:T(8,128)(2,1)} %blocks.1), custom_call_target="tpu_custom_call" | custom-call | bytes 9437184 | tf_op jit(solution)/shard_map/arrange/pallas_call | solution.py:87
  10.2 0.0 copy-start
  10.3 1.1 %copy-done = bf16[2048,384]{1,0:T(8,128)(2,1)} copy-done((bf16[2048,384]{1,0:T(8,128)(2,1)}, bf16[2048,384]{1,0:T(8,128)(2,1)S(1)}, u32[]{:S(2)}) %copy-start) | copy-done | bytes 1572888
  11.4 5.6 %all-to-all-done.blocks = bf16[16,128,128]{2,1,0:T(8,128)(2,1)} async-done(((bf16[16,128,128]{2,1,0:T(8,128)(2,1)}), bf16[16,128,128]{2,1,0:T(8,128)(2,1)}, u32[]{:S(2)}, u32[]{:S(2)}) %all-to-all-start) | async-done | bytes 524320 | tf_op jit(solution)/shard_map/all_to_all | solution.py:224
  17.0 1.3 %place.1 = bf16[128,2048]{1,0:T(8,128)(2,1)S(1)} custom-call(bf16[128,128]{1,0:T(8,128)(2,1)S(1)} %get-tuple-element.10.pick, bf16[16,128,128]{2,1,0:T(8,128)(2,1)} %all-to-all-done.blocks, bf16[2048,208]{1,0:T(8,128)(2,1)S(1)} %get-tuple-element.11._.modes), custom_call_target="tpu_custom_call" | custom-call | tf_op jit(solution)/shard_map/place/pallas_call | solution.py:190
  18.4 0.1 collective-permute-start.4
  18.5 2.4 %collective-permute-start.1 = (bf16[16,2048]{1,0:T(8,128)(2,1)S(1)}, bf16[16,2048]{1,0:T(8,128)(2,1)S(1)}, u32[]{:S(2)}, u32[]{:S(2)}) collective-permute-start(bf16[16,2048]{1,0:T(8,128)(2,1)S(1)} %slice.35), channel_id=1, source_target_pairs={{0,24},{1,25},{2,26},{3,27},{4,28},{5,29},{6,30},{7,31},{8,16},{9,... | collective-permute-start | bytes 196616 | tf_op jit(solution)/shard_map/ppermute | solution.py:45
  20.8 0.5 collective-permute-start.15
  21.4 2.6 %collective-permute-done.1.refs_1_.refs_5_ = bf16[16,2048]{1,0:T(8,128)(2,1)S(1)} collective-permute-done((bf16[16,2048]{1,0:T(8,128)(2,1)S(1)}, bf16[16,2048]{1,0:T(8,128)(2,1)S(1)}, u32[]{:S(2)}, u32[]{:S(2)}) %collective-permute-start.1) | collective-permute-done | bytes 65568 | tf_op jit(solution)/shard_map/ppermute | solution.py:45
  24.0 1.5 %collective-permute-start.7 = (bf16[48,2048]{1,0:T(8,128)(2,1)S(1)}, bf16[48,2048]{1,0:T(8,128)(2,1)S(1)}, u32[]{:S(2)}, u32[]{:S(2)}) collective-permute-start(bf16[48,2048]{1,0:T(8,128)(2,1)S(1)} %get-tuple-element.14), channel_id=1, source_target_pairs={{0,6},{1,7},{2,4},{3,5},{4,2},{5,3},{6,0},{7,1},{8,14},{9,15},{10,... | collective-permute-start | bytes 589832 | tf_op jit(solution)/shard_map/ppermute | solution.py:45
  25.5 0.3 collective-permute-start.22
  25.8 1.5 %collective-permute-start = (bf16[32,2048]{1,0:T(8,128)(2,1)S(1)}, bf16[32,2048]{1,0:T(8,128)(2,1)S(1)}, u32[]{:S(2)}, u32[]{:S(2)}) collective-permute-start(bf16[32,2048]{1,0:T(8,128)(2,1)S(1)} %slice.34), channel_id=1, source_target_pairs={{0,8},{1,9},{2,10},{3,11},{4,12},{5,13},{6,14},{7,15},{8,0},{9,1},... | collective-permute-start | bytes 393224 | tf_op jit(solution)/shard_map/ppermute | solution.py:45
  27.3 1.6 %collective-permute-start.6 = (bf16[64,2048]{1,0:T(8,128)(2,1)S(1)}, bf16[64,2048]{1,0:T(8,128)(2,1)S(1)}, u32[]{:S(2)}, u32[]{:S(2)}) collective-permute-start(bf16[64,2048]{1,0:T(8,128)(2,1)S(1)} %slice.38), channel_id=1, source_target_pairs={{0,2},{1,3},{2,0},{3,1},{4,6},{5,7},{6,4},{7,5},{8,10},{9,11},{10,... | collective-permute-start | bytes 786440 | tf_op jit(solution)/shard_map/ppermute | solution.py:45
  28.9 2.6 %collective-permute-done.refs_0_.refs_3_ = bf16[32,2048]{1,0:T(8,128)(2,1)S(1)} collective-permute-done((bf16[32,2048]{1,0:T(8,128)(2,1)S(1)}, bf16[32,2048]{1,0:T(8,128)(2,1)S(1)}, u32[]{:S(2)}, u32[]{:S(2)}) %collective-permute-start) | collective-permute-done | bytes 131104 | tf_op jit(solution)/shard_map/ppermute | solution.py:45
  31.5 2.7 %collective-permute-start.9 = (bf16[16,2048]{1,0:T(8,128)(2,1)S(1)}, bf16[16,2048]{1,0:T(8,128)(2,1)S(1)}, u32[]{:S(2)}, u32[]{:S(2)}) collective-permute-start(bf16[16,2048]{1,0:T(8,128)(2,1)S(1)} %slice.39), channel_id=1, source_target_pairs={{0,24},{1,25},{2,26},{3,27},{4,28},{5,29},{6,30},{7,31},{8,16},{9,... | collective-permute-start | bytes 196616 | tf_op jit(solution)/shard_map/ppermute | solution.py:45
  34.2 0.8 %collective-permute-start.2 = (bf16[48,2048]{1,0:T(8,128)(2,1)S(1)}, bf16[48,2048]{1,0:T(8,128)(2,1)S(1)}, u32[]{:S(2)}, u32[]{:S(2)}) collective-permute-start(bf16[48,2048]{1,0:T(8,128)(2,1)S(1)} %shard_map.46), channel_id=1, source_target_pairs={{0,2},{1,3},{2,0},{3,1},{4,6},{5,7},{6,4},{7,5},{8,10},{9,11},{10,... | collective-permute-start | bytes 589832 | tf_op jit(solution)/shard_map/ppermute | solution.py:45
  35.0 1.6 %collective-permute-done.9.refs_4_ = bf16[16,2048]{1,0:T(8,128)(2,1)S(1)} collective-permute-done((bf16[16,2048]{1,0:T(8,128)(2,1)S(1)}, bf16[16,2048]{1,0:T(8,128)(2,1)S(1)}, u32[]{:S(2)}, u32[]{:S(2)}) %collective-permute-start.9) | collective-permute-done | bytes 65568 | tf_op jit(solution)/shard_map/ppermute | solution.py:45
  36.6 1.5 %collective-permute-start.5 = (bf16[32,2048]{1,0:T(8,128)(2,1)S(1)}, bf16[32,2048]{1,0:T(8,128)(2,1)S(1)}, u32[]{:S(2)}, u32[]{:S(2)}) collective-permute-start(bf16[32,2048]{1,0:T(8,128)(2,1)S(1)} %slice.37), channel_id=1, source_target_pairs={{0,8},{1,9},{2,10},{3,11},{4,12},{5,13},{6,14},{7,15},{8,0},{9,1},... | collective-permute-start | bytes 393224 | tf_op jit(solution)/shard_map/ppermute | solution.py:45
  38.1 1.9 %collective-permute-start.3 = (bf16[48,2048]{1,0:T(8,128)(2,1)S(1)}, bf16[48,2048]{1,0:T(8,128)(2,1)S(1)}, u32[]{:S(2)}, u32[]{:S(2)}) collective-permute-start(bf16[48,2048]{1,0:T(8,128)(2,1)S(1)} %shard_map.46), channel_id=1, source_target_pairs={{0,6},{1,7},{2,4},{3,5},{4,2},{5,3},{6,0},{7,1},{8,14},{9,15},{10,... | collective-permute-start | bytes 589832 | tf_op jit(solution)/shard_map/ppermute | solution.py:45
  40.0 0.2 collective-permute-start.18
  40.3 1.3 %collective-permute-done.5.refs_2_ = bf16[32,2048]{1,0:T(8,128)(2,1)S(1)} collective-permute-done((bf16[32,2048]{1,0:T(8,128)(2,1)S(1)}, bf16[32,2048]{1,0:T(8,128)(2,1)S(1)}, u32[]{:S(2)}, u32[]{:S(2)}) %collective-permute-start.5) | collective-permute-done | bytes 131104 | tf_op jit(solution)/shard_map/ppermute | solution.py:45
  41.6 1.8 %collective-permute-start.8 = (bf16[48,2048]{1,0:T(8,128)(2,1)S(1)}, bf16[48,2048]{1,0:T(8,128)(2,1)S(1)}, u32[]{:S(2)}, u32[]{:S(2)}) collective-permute-start(bf16[48,2048]{1,0:T(8,128)(2,1)S(1)} %shard_map.47), channel_id=1, source_target_pairs={{0,16},{1,17},{2,18},{3,19},{4,20},{5,21},{6,22},{7,23},{8,24},{9,... | collective-permute-start | bytes 589832 | tf_op jit(solution)/shard_map/ppermute | solution.py:45
  43.4 2.3 %shard_map.48.refs_12_ = f32[2048,2048]{1,0:T(8,128)S(1)} custom-call(bf16[2048,208]{1,0:T(8,128)(2,1)S(1)} %get-tuple-element.11._.modes, bf16[48,2048]{1,0:T(8,128)(2,1)S(1)} %get-tuple-element.13.refs_0_, bf16[80,2048]{1,0:T(8,128)(2,1)S(1)} %slice.41.refs_1_, bf16[80,2048]{1,0:T(8,128)(2,1)S(1)} %collective-permute-done.22.refs_2_), custom_call_target="tpu_custom_call" | custom-call | flops 1744830464 | bytes 8388608 | tf_op jit(solution)/shard_map/pallas_call | solution.py:161
  45.8 1.0 %collective-permute-done.3.refs_1_ = bf16[48,2048]{1,0:T(8,128)(2,1)S(1)} collective-permute-done((bf16[48,2048]{1,0:T(8,128)(2,1)S(1)}, bf16[48,2048]{1,0:T(8,128)(2,1)S(1)}, u32[]{:S(2)}, u32[]{:S(2)}) %collective-permute-start.3) | collective-permute-done | bytes 196640 | tf_op jit(solution)/shard_map/ppermute | solution.py:45
  46.7 0.5 collective-permute-start.12
  47.2 0.1 collective-permute-start.10
  47.3 1.6 %collective-permute-done.8.refs_3_ = bf16[48,2048]{1,0:T(8,128)(2,1)S(1)} collective-permute-done((bf16[48,2048]{1,0:T(8,128)(2,1)S(1)}, bf16[48,2048]{1,0:T(8,128)(2,1)S(1)}, u32[]{:S(2)}, u32[]{:S(2)}) %collective-permute-start.8) | collective-permute-done | bytes 196640 | tf_op jit(solution)/shard_map/ppermute | solution.py:45
  49.0 0.5 collective-permute-start.13
  49.5 5.2 %shard_map.49.refs_10_ = f32[2048,2048]{1,0:T(8,128)S(1)} custom-call(bf16[2048,448]{1,0:T(8,128)(2,1)S(1)} %get-tuple-element.12.modes, bf16[64,2048]{1,0:T(8,128)(2,1)S(1)} %collective-permute-done.6.refs_0_, bf16[48,2048]{1,0:T(8,128)(2,1)S(1)} %collective-permute-done.7.refs_1_, ...), custom_call_target="tpu_custom_call", output_to_operand_aliasing={{}: (13, {})} | custom-call | flops 3758096384 | bytes 8388608 | tf_op jit(solution)/shard_map/pallas_call | solution.py:161
  54.8 5.9 %shard_map.50 = bf16[2048,2048]{1,0:T(8,128)(2,1)} custom-call(bf16[2048,384]{1,0:T(8,128)(2,1)S(1)} %copy-done.1, bf16[48,2048]{1,0:T(8,128)(2,1)S(1)} %collective-permute-done.2.refs_0_, bf16[48,2048]{1,0:T(8,128)(2,1)S(1)} %collective-permute-done.3.refs_1_, bf16[32,2048]{1,0:T(8,128)(2,1)S(1)} %collective-permute-done.5.refs_2_, ...), custom_call_target="tpu_custom_call" | custom-call | flops 3221225472 | bytes 8388608 | tf_op jit(solution)/shard_map/pallas_call | solution.py:161
  (36 shorter events, 0.2 us)
Async XLA Ops:
  0.0 17.0 %all-to-all-start = ((bf16[16,128,128]{2,1,0:T(8,128)(2,1)}), bf16[16,128,128]{2,1,0:T(8,128)(2,1)}, u32[]{:S(2)}, u32[]{:S(2)}) async-start(bf16[16,128,128]{2,1,0:T(8,128)(2,1)} %bitcast.1), calls=%async_computation | async-start | bytes 1048576 | tf_op jit(solution)/shard_map/all_to_all | solution.py:224
  6.7 0.7 %copy-start.2 = (s32[1,128]{1,0:T(1,128)S(1)}, s32[1,128]{1,0:T(1,128)}, u32[]{:S(2)}) copy-start(s32[1,128]{1,0:T(1,128)} %slots.1) | copy-start | bytes 1540
  10.2 1.1 %copy-start = (bf16[2048,384]{1,0:T(8,128)(2,1)}, bf16[2048,384]{1,0:T(8,128)(2,1)S(1)}, u32[]{:S(2)}) copy-start(bf16[2048,384]{1,0:T(8,128)(2,1)S(1)} %get-tuple-element.9.modes) | copy-start | bytes 4718596
  18.4 10.5 %collective-permute-start.4 = (bf16[48,2048]{1,0:T(8,128)(2,1)S(1)}, bf16[48,2048]{1,0:T(8,128)(2,1)S(1)}, u32[]{:S(2)}, u32[]{:S(2)}) collective-permute-start(bf16[48,2048]{1,0:T(8,128)(2,1)S(1)} %get-tuple-element.14), channel_id=1, source_target_pairs={{0,4},{1,5},{2,6},{3,7},{4,0},{5,1},{6,2},{7,3},{8,12},{9,13},{10,... | collective-permute-start | bytes 589832 | tf_op jit(solution)/shard_map/ppermute | solution.py:45
  18.5 5.5 %collective-permute-start.1 = (bf16[16,2048]{1,0:T(8,128)(2,1)S(1)}, bf16[16,2048]{1,0:T(8,128)(2,1)S(1)}, u32[]{:S(2)}, u32[]{:S(2)}) collective-permute-start(bf16[16,2048]{1,0:T(8,128)(2,1)S(1)} %slice.35), channel_id=1, source_target_pairs={{0,24},{1,25},{2,26},{3,27},{4,28},{5,29},{6,30},{7,31},{8,16},{9,... | collective-permute-start | bytes 196616 | tf_op jit(solution)/shard_map/ppermute | solution.py:45
  20.8 5.0 %collective-permute-start.15 = (bf16[16,2048]{1,0:T(8,128)(2,1)S(1)}, bf16[16,2048]{1,0:T(8,128)(2,1)S(1)}, u32[]{:S(2)}, u32[]{:S(2)}) collective-permute-start(bf16[16,2048]{1,0:T(8,128)(2,1)S(1)} %slice.35), channel_id=1, source_target_pairs={{0,16},{1,17},{2,18},{3,19},{4,20},{5,21},{6,22},{7,23},{8,24},{9,... | collective-permute-start | bytes 196616 | tf_op jit(solution)/shard_map/ppermute | solution.py:45
  23.9 3.3 %collective-permute-start.21 = (bf16[16,2048]{1,0:T(8,128)(2,1)S(1)}, bf16[16,2048]{1,0:T(8,128)(2,1)S(1)}, u32[]{:S(2)}, u32[]{:S(2)}) collective-permute-start(bf16[16,2048]{1,0:T(8,128)(2,1)S(1)} %collective-permute-done.1.refs_1_.refs_5_), channel_id=1, source_target_pairs={{0,1},{1,0},{2,3},{3,2},{4,5},{5,4},{6,7},{7,6},{8,9},{9,8},{10,11... | collective-permute-start | bytes 196616 | tf_op jit(solution)/shard_map/ppermute | solution.py:45
  24.0 11.1 %collective-permute-start.7 = (bf16[48,2048]{1,0:T(8,128)(2,1)S(1)}, bf16[48,2048]{1,0:T(8,128)(2,1)S(1)}, u32[]{:S(2)}, u32[]{:S(2)}) collective-permute-start(bf16[48,2048]{1,0:T(8,128)(2,1)S(1)} %get-tuple-element.14), channel_id=1, source_target_pairs={{0,6},{1,7},{2,4},{3,5},{4,2},{5,3},{6,0},{7,1},{8,14},{9,15},{10,... | collective-permute-start | bytes 589832 | tf_op jit(solution)/shard_map/ppermute | solution.py:45
  25.5 14.6 %collective-permute-start.22 = (bf16[80,2048]{1,0:T(8,128)(2,1)S(1)}, bf16[80,2048]{1,0:T(8,128)(2,1)S(1)}, u32[]{:S(2)}, u32[]{:S(2)}) collective-permute-start(bf16[80,2048]{1,0:T(8,128)(2,1)S(1)} %slice.41.refs_1_), channel_id=1, source_target_pairs={{0,1},{1,0},{2,3},{3,2},{4,5},{5,4},{6,7},{7,6},{8,9},{9,8},{10,11... | collective-permute-start | bytes 983048 | tf_op jit(solution)/shard_map/ppermute | solution.py:45
  25.8 5.7 %collective-permute-start = (bf16[32,2048]{1,0:T(8,128)(2,1)S(1)}, bf16[32,2048]{1,0:T(8,128)(2,1)S(1)}, u32[]{:S(2)}, u32[]{:S(2)}) collective-permute-start(bf16[32,2048]{1,0:T(8,128)(2,1)S(1)} %slice.34), channel_id=1, source_target_pairs={{0,8},{1,9},{2,10},{3,11},{4,12},{5,13},{6,14},{7,15},{8,0},{9,1},... | collective-permute-start | bytes 393224 | tf_op jit(solution)/shard_map/ppermute | solution.py:45
  27.3 10.8 %collective-permute-start.6 = (bf16[64,2048]{1,0:T(8,128)(2,1)S(1)}, bf16[64,2048]{1,0:T(8,128)(2,1)S(1)}, u32[]{:S(2)}, u32[]{:S(2)}) collective-permute-start(bf16[64,2048]{1,0:T(8,128)(2,1)S(1)} %slice.38), channel_id=1, source_target_pairs={{0,2},{1,3},{2,0},{3,1},{4,6},{5,7},{6,4},{7,5},{8,10},{9,11},{10,... | collective-permute-start | bytes 786440 | tf_op jit(solution)/shard_map/ppermute | solution.py:45
  28.9 5.3 %collective-permute-start.20 = (bf16[16,2048]{1,0:T(8,128)(2,1)S(1)}, bf16[16,2048]{1,0:T(8,128)(2,1)S(1)}, u32[]{:S(2)}, u32[]{:S(2)}) collective-permute-start(bf16[16,2048]{1,0:T(8,128)(2,1)S(1)} %collective-permute-done.15.refs_4_), channel_id=1, source_target_pairs={{0,1},{1,0},{2,3},{3,2},{4,5},{5,4},{6,7},{7,6},{8,9},{9,8},{10,11... | collective-permute-start | bytes 196616 | tf_op jit(solution)/shard_map/ppermute | solution.py:45
  31.5 5.2 %collective-permute-start.9 = (bf16[16,2048]{1,0:T(8,128)(2,1)S(1)}, bf16[16,2048]{1,0:T(8,128)(2,1)S(1)}, u32[]{:S(2)}, u32[]{:S(2)}) collective-permute-start(bf16[16,2048]{1,0:T(8,128)(2,1)S(1)} %slice.39), channel_id=1, source_target_pairs={{0,24},{1,25},{2,26},{3,27},{4,28},{5,29},{6,30},{7,31},{8,16},{9,... | collective-permute-start | bytes 196616 | tf_op jit(solution)/shard_map/ppermute | solution.py:45
  34.2 7.4 %collective-permute-start.2 = (bf16[48,2048]{1,0:T(8,128)(2,1)S(1)}, bf16[48,2048]{1,0:T(8,128)(2,1)S(1)}, u32[]{:S(2)}, u32[]{:S(2)}) collective-permute-start(bf16[48,2048]{1,0:T(8,128)(2,1)S(1)} %shard_map.46), channel_id=1, source_target_pairs={{0,2},{1,3},{2,0},{3,1},{4,6},{5,7},{6,4},{7,5},{8,10},{9,11},{10,... | collective-permute-start | bytes 589832 | tf_op jit(solution)/shard_map/ppermute | solution.py:45
  35.0 3.1 %collective-permute-start.19 = (bf16[32,2048]{1,0:T(8,128)(2,1)S(1)}, bf16[32,2048]{1,0:T(8,128)(2,1)S(1)}, u32[]{:S(2)}, u32[]{:S(2)}) collective-permute-start(bf16[32,2048]{1,0:T(8,128)(2,1)S(1)} %collective-permute-done.refs_0_.refs_3_), channel_id=1, source_target_pairs={{0,1},{1,0},{2,3},{3,2},{4,5},{5,4},{6,7},{7,6},{8,9},{9,8},{10,11... | collective-permute-start | bytes 393224 | tf_op jit(solution)/shard_map/ppermute | solution.py:45
  36.6 5.0 %collective-permute-start.5 = (bf16[32,2048]{1,0:T(8,128)(2,1)S(1)}, bf16[32,2048]{1,0:T(8,128)(2,1)S(1)}, u32[]{:S(2)}, u32[]{:S(2)}) collective-permute-start(bf16[32,2048]{1,0:T(8,128)(2,1)S(1)} %slice.37), channel_id=1, source_target_pairs={{0,8},{1,9},{2,10},{3,11},{4,12},{5,13},{6,14},{7,15},{8,0},{9,1},... | collective-permute-start | bytes 393224 | tf_op jit(solution)/shard_map/ppermute | solution.py:45
  38.1 10.9 %collective-permute-start.16 = (bf16[64,2048]{1,0:T(8,128)(2,1)S(1)}, bf16[64,2048]{1,0:T(8,128)(2,1)S(1)}, u32[]{:S(2)}, u32[]{:S(2)}) collective-permute-start(bf16[64,2048]{1,0:T(8,128)(2,1)S(1)} %collective-permute-done.6.refs_0_), channel_id=1, source_target_pairs={{0,1},{1,0},{2,3},{3,2},{4,5},{5,4},{6,7},{7,6},{8,9},{9,8},{10,11... | collective-permute-start | bytes 786440 | tf_op jit(solution)/shard_map/ppermute | solution.py:45
  38.1 8.6 %collective-permute-start.3 = (bf16[48,2048]{1,0:T(8,128)(2,1)S(1)}, bf16[48,2048]{1,0:T(8,128)(2,1)S(1)}, u32[]{:S(2)}, u32[]{:S(2)}) collective-permute-start(bf16[48,2048]{1,0:T(8,128)(2,1)S(1)} %shard_map.46), channel_id=1, source_target_pairs={{0,6},{1,7},{2,4},{3,5},{4,2},{5,3},{6,0},{7,1},{8,14},{9,15},{10,... | collective-permute-start | bytes 589832 | tf_op jit(solution)/shard_map/ppermute | solution.py:45
  40.0 6.7 %collective-permute-start.18 = (bf16[48,2048]{1,0:T(8,128)(2,1)S(1)}, bf16[48,2048]{1,0:T(8,128)(2,1)S(1)}, u32[]{:S(2)}, u32[]{:S(2)}) collective-permute-start(bf16[48,2048]{1,0:T(8,128)(2,1)S(1)} %collective-permute-done.4.refs_2_), channel_id=1, source_target_pairs={{0,1},{1,0},{2,3},{3,2},{4,5},{5,4},{6,7},{7,6},{8,9},{9,8},{10,11... | collective-permute-start | bytes 589832 | tf_op jit(solution)/shard_map/ppermute | solution.py:45
  41.6 5.6 %collective-permute-start.17 = (bf16[48,2048]{1,0:T(8,128)(2,1)S(1)}, bf16[48,2048]{1,0:T(8,128)(2,1)S(1)}, u32[]{:S(2)}, u32[]{:S(2)}) collective-permute-start(bf16[48,2048]{1,0:T(8,128)(2,1)S(1)} %collective-permute-done.7.refs_1_), channel_id=1, source_target_pairs={{0,1},{1,0},{2,3},{3,2},{4,5},{5,4},{6,7},{7,6},{8,9},{9,8},{10,11... | collective-permute-start | bytes 589832 | tf_op jit(solution)/shard_map/ppermute | solution.py:45
  41.6 7.4 %collective-permute-start.8 = (bf16[48,2048]{1,0:T(8,128)(2,1)S(1)}, bf16[48,2048]{1,0:T(8,128)(2,1)S(1)}, u32[]{:S(2)}, u32[]{:S(2)}) collective-permute-start(bf16[48,2048]{1,0:T(8,128)(2,1)S(1)} %shard_map.47), channel_id=1, source_target_pairs={{0,16},{1,17},{2,18},{3,19},{4,20},{5,21},{6,22},{7,23},{8,24},{9,... | collective-permute-start | bytes 589832 | tf_op jit(solution)/shard_map/ppermute | solution.py:45
  46.7 8.0 %collective-permute-start.14 = (bf16[16,2048]{1,0:T(8,128)(2,1)S(1)}, bf16[16,2048]{1,0:T(8,128)(2,1)S(1)}, u32[]{:S(2)}, u32[]{:S(2)}) collective-permute-start(bf16[16,2048]{1,0:T(8,128)(2,1)S(1)} %collective-permute-done.9.refs_4_), channel_id=1, source_target_pairs={{0,1},{1,0},{2,3},{3,2},{4,5},{5,4},{6,7},{7,6},{8,9},{9,8},{10,11... | collective-permute-start | bytes 196616 | tf_op jit(solution)/shard_map/ppermute | solution.py:45
  46.7 8.0 %collective-permute-start.12 = (bf16[32,2048]{1,0:T(8,128)(2,1)S(1)}, bf16[32,2048]{1,0:T(8,128)(2,1)S(1)}, u32[]{:S(2)}, u32[]{:S(2)}) collective-permute-start(bf16[32,2048]{1,0:T(8,128)(2,1)S(1)} %collective-permute-done.5.refs_2_), channel_id=1, source_target_pairs={{0,1},{1,0},{2,3},{3,2},{4,5},{5,4},{6,7},{7,6},{8,9},{9,8},{10,11... | collective-permute-start | bytes 393224 | tf_op jit(solution)/shard_map/ppermute | solution.py:45
  47.2 7.5 %collective-permute-start.10 = (bf16[48,2048]{1,0:T(8,128)(2,1)S(1)}, bf16[48,2048]{1,0:T(8,128)(2,1)S(1)}, u32[]{:S(2)}, u32[]{:S(2)}) collective-permute-start(bf16[48,2048]{1,0:T(8,128)(2,1)S(1)} %collective-permute-done.2.refs_0_), channel_id=1, source_target_pairs={{0,1},{1,0},{2,3},{3,2},{4,5},{5,4},{6,7},{7,6},{8,9},{9,8},{10,11... | collective-permute-start | bytes 589832 | tf_op jit(solution)/shard_map/ppermute | solution.py:45
  49.0 5.8 %collective-permute-start.11 = (bf16[48,2048]{1,0:T(8,128)(2,1)S(1)}, bf16[48,2048]{1,0:T(8,128)(2,1)S(1)}, u32[]{:S(2)}, u32[]{:S(2)}) collective-permute-start(bf16[48,2048]{1,0:T(8,128)(2,1)S(1)} %collective-permute-done.3.refs_1_), channel_id=1, source_target_pairs={{0,1},{1,0},{2,3},{3,2},{4,5},{5,4},{6,7},{7,6},{8,9},{9,8},{10,11... | collective-permute-start | bytes 589832 | tf_op jit(solution)/shard_map/ppermute | solution.py:45
  49.0 5.8 %collective-permute-start.13 = (bf16[48,2048]{1,0:T(8,128)(2,1)S(1)}, bf16[48,2048]{1,0:T(8,128)(2,1)S(1)}, u32[]{:S(2)}, u32[]{:S(2)}) collective-permute-start(bf16[48,2048]{1,0:T(8,128)(2,1)S(1)} %collective-permute-done.8.refs_3_), channel_id=1, source_target_pairs={{0,1},{1,0},{2,3},{3,2},{4,5},{5,4},{6,7},{7,6},{8,9},{9,8},{10,11... | collective-permute-start | bytes 589832 | tf_op jit(solution)/shard_map/ppermute | solution.py:45
  49.5 5.3 %copy-start.1 = (bf16[2048,384]{1,0:T(8,128)(2,1)S(1)}, bf16[2048,384]{1,0:T(8,128)(2,1)}, u32[]{:S(2)}) copy-start(bf16[2048,384]{1,0:T(8,128)(2,1)} %copy-done) | copy-start | bytes 4718596
